TPU v7x, 256 devices: a whole 4x4x8 slice. The times are simulated.
256 devices in a mesh: loop: 16 (over z, y_lo), rep: 16 (over y_hi, x, core).
Axes of the slice: x: 4, y: 4 (y_hi: 2, y_lo: 2; y = y_hi * 2 + y_lo), z: 8, core: 2. Of those that a mesh axis runs over, the one named last changes fastest.
Arguments:
- features: bfloat16 [65536, 128], P(('loop', 'rep')), may hold values from -6 to 6
- w_self: bfloat16 [128, 256], replicated, may hold values from -0.5 to 0.5
- w_neigh: bfloat16 [128, 256], replicated, may hold values from -0.5 to 0.5
- bias: float32 [256], replicated, may hold values from -3 to 3
- degree: int32 [65536], P(('loop', 'rep')), may hold values from 1 to 4
- tiles: bfloat16 [16, 16, 16, 16, 128, 128], P('loop', 'rep'), may hold values from -0.0625 to 0.0625
- dst_block: int32 [16, 16, 16, 16], P('loop', 'rep'), may hold values from 0 to 31, as said below
- src_block: int32 [16, 16, 16, 16], P('loop', 'rep'), may hold values from 0 to 1, as said below
- live_count: int32 [16, 16, 16], P('loop', 'rep'), may hold values from 1 to 16, as said below
- cotangent: bfloat16 [65536, 256], P(('loop', 'rep')), may hold values from -6 to 6
Outputs:
- output: bfloat16 [65536, 256], P(('loop', 'rep'))
- grad_input: bfloat16 [65536, 128], P(('loop', 'rep'))
- grad_self: float32 [128, 256], replicated
- grad_neigh: float32 [128, 256], replicated
- grad_bias: float32 [256], replicated
Inputs may be any that keep to these rules, and one draw needn't show every extreme that they name: Within one (p, r, q) the 16 slots name distinct pairs (dst_block, src_block). Within one (p, r, q) the 16 slots name distinct pairs (dst_block, src_block). `live_count`: every device (p, r) has some q with all 16 slots live; slots at or past the count hold tiles that are not part of the graph.
All inputs are finite; a program needn't handle non-finite values.
Results may differ from a plain program's by a relative error of at most 0.0075.
Values may be sent and summed in bfloat16 or wider, within the bound.
A program may use at most 128 MiB of HBM per device.

v0:
```python
import math
import jax
import jax.numpy as jnp
from jax import lax
from jax.sharding import PartitionSpec as P


def shifted(block, axis, distance):
    devices = range(lax.axis_size(axis))
    route = [((i - distance) % len(devices), i) for i in devices]
    return lax.ppermute(block, axis, route)


def per_device(
    features, w_self, w_neigh, bias, degree, tiles, dst_block, src_block, live_count, cotangent
):
    loop_count = lax.axis_size("loop")
    rep_count = lax.axis_size("rep")
    loop_here = lax.axis_index("loop")
    row_count, feat_width = features.shape
    tile_size = tiles.shape[-1]
    slot_count = tiles.shape[3]
    sub_blocks = row_count // tile_size
    row_blocks = sub_blocks * rep_count
    tile_all = tiles[0, 0]
    dst_all = dst_block[0, 0]
    src_all = src_block[0, 0]
    live_all = jnp.arange(slot_count)[None, :] < live_count[0, 0][:, None]
    place_all = (
        (dst_all[:, :, None] == jnp.arange(row_blocks)[None, None, :]) & live_all[:, :, None]
    ).astype(jnp.float32)
    land_all = (
        (src_all[:, :, None] == jnp.arange(sub_blocks)[None, None, :]) & live_all[:, :, None]
    ).astype(jnp.float32)

    def pick_entry(table, source):
        return lax.dynamic_index_in_dim(table, source, 0, keepdims=False)

    def gather_term(source, panel):
        tile_part = pick_entry(tile_all, source)
        chosen = jnp.take(
            panel.reshape(sub_blocks, tile_size, feat_width), pick_entry(src_all, source), axis=0
        )
        product = jnp.einsum("tij,tjf->tif", tile_part, chosen, preferred_element_type=jnp.float32)
        return jnp.einsum(
            "td,tif->dif", pick_entry(place_all, source), product, precision=lax.Precision.HIGHEST
        )

    running = gather_term(loop_here, features)

    def one_way(step_index, state):
        panel, total = state
        panel = shifted(panel, "loop", 1)
        return (panel, total + gather_term((loop_here - step_index) % loop_count, panel))

    _, running = lax.fori_loop(1, loop_count, one_way, (features, running))
    agg_sum = lax.psum_scatter(
        running.reshape(row_blocks * tile_size, feat_width), "rep", scatter_dimension=0, tiled=True
    )
    degree_f = degree.astype(jnp.float32)[:, None]
    aggregate = (agg_sum / degree_f).astype(jnp.bfloat16)
    preact = (
        jnp.dot(features, w_self, preferred_element_type=jnp.float32)
        + jnp.dot(aggregate, w_neigh, preferred_element_type=jnp.float32)
        + bias
    )
    sigmoid_val = jax.nn.sigmoid(preact)
    output = (preact * sigmoid_val).astype(jnp.bfloat16)
    grad_pre = (
        cotangent.astype(jnp.float32) * sigmoid_val * (1.0 + preact * (1.0 - sigmoid_val))
    ).astype(jnp.bfloat16)
    grad_agg = (
        jnp.einsum("nh,fh->nf", grad_pre, w_neigh, preferred_element_type=jnp.float32) / degree_f
    ).astype(jnp.bfloat16)
    grad_whole = lax.all_gather(grad_agg, "rep", axis=0, tiled=True).reshape(
        row_blocks, tile_size, feat_width
    )
    node_total = row_count * loop_count * rep_count
    grad_scale = 1.0 / math.sqrt(node_total)
    grad_self, grad_neigh, grad_bias = lax.psum(
        (
            jnp.einsum("nf,nh->fh", features, grad_pre, preferred_element_type=jnp.float32)
            * grad_scale,
            jnp.einsum("nf,nh->fh", aggregate, grad_pre, preferred_element_type=jnp.float32)
            * grad_scale,
            jnp.sum(grad_pre.astype(jnp.float32), axis=0) * grad_scale,
        ),
        ("loop", "rep"),
    )
    self_grad = jnp.einsum("nh,fh->nf", grad_pre, w_self, preferred_element_type=jnp.float32)

    def spread_term(source):
        tile_part = pick_entry(tile_all, source)
        chosen = jnp.take(grad_whole, pick_entry(dst_all, source), axis=0)
        product = jnp.einsum("tij,tif->tjf", tile_part, chosen, preferred_element_type=jnp.float32)
        summed = jnp.einsum(
            "ts,tjf->sjf", pick_entry(land_all, source), product, precision=lax.Precision.HIGHEST
        )
        return summed.reshape(row_count, feat_width)

    def carry_along(step_index, total):
        total = shifted(total, "loop", -1)
        return total + spread_term((loop_here + 1 + step_index) % loop_count)

    neigh_grad = lax.fori_loop(
        1, loop_count, carry_along, spread_term((loop_here + 1) % loop_count)
    )
    grad_input = (self_grad + neigh_grad).astype(jnp.bfloat16)
    return (output, grad_input, grad_self, grad_neigh, grad_bias)


def solution(mesh):
    in_specs = (
        P(("loop", "rep"), None),
        P(),
        P(),
        P(),
        P(("loop", "rep")),
        P("loop", "rep", None, None, None, None),
        P("loop", "rep", None, None),
        P("loop", "rep", None, None),
        P("loop", "rep", None),
        P(("loop", "rep"), None),
    )
    out_specs = (P(("loop", "rep"), None), P(("loop", "rep"), None), P(), P(), P())
    return jax.shard_map(
        per_device, mesh=mesh, in_specs=in_specs, out_specs=out_specs, check_vma=False
    )
```

profile of v0, /device:TPU:2, one launch (start us, length us, event | category | flops | bytes accessed | tf_op | source)
XLA Modules:
  0.0 704.0 jit_solution(3189512164626604518)
XLA Ops:
  14.8 174.0 %while.32 = (s32[]{:T(128)}, bf16[256,128]{1,0:T(8,128)(2,1)S(1)}, f32[32,128,128]{2,0,1:T(8,128)S(1)}, s32[]{:T(128)}, f32[16,16,32]{2,1,0:T(8,128)S(1)}, /*ind...) while((s32[]{:T(128)}, bf16[256,128]{1,0:T(8,128)(2,1)S(1)}, ...), condition=%wide.region_1.3_spmd, body=%wide.region_0.2_spmd.sunk | while | flops 168559728 | bytes 8794716 | solution.py:56
  16.5 7.5 %collective-permute-done = bf16[256,128]{1,0:T(8,128)(2,1)S(1)} collective-permute-done((bf16[256,128]{1,0:T(8,128)(2,1)S(1)}, bf16[256,128]{1,0:T(8,128)(2,1)S(1)}, u32[]{:S(2)}, u32[]{:S(2)}) %collective-permute-start) | collective-permute-done | bytes 65568 | tf_op jit(solution)/shard_map/while/body/eval_jaxpr/ppermute | solution.py:11
  29.1 6.3 collective-permute-done
  40.5 6.3 collective-permute-done
  51.8 6.3 collective-permute-done
  63.2 6.3 collective-permute-done
  74.6 6.3 collective-permute-done
  86.0 6.3 collective-permute-done
  97.4 6.3 collective-permute-done
  108.8 6.8 collective-permute-done
  120.7 6.3 collective-permute-done
  132.0 6.3 collective-permute-done
  143.4 6.3 collective-permute-done
  154.8 6.3 collective-permute-done
  166.2 6.3 collective-permute-done
  177.6 6.3 collective-permute-done
  192.4 77.7 %reduce-scatter.2.cloned.1.call-done = f32[256,128]{1,0:T(8,128)} async-done(((f32[4096,128]{1,0:T(8,128)}), f32[256,128]{1,0:T(8,128)}) %reduce-scatter.2.cloned.1.call-update) | async-done | bytes 131088 | tf_op jit(solution)/shard_map/reduce_scatter | solution.py:57
  275.6 74.1 %psum.23 = f32[256]{0:T(256)} all-reduce(f32[256]{0:T(256)S(1)} %broadcast_multiply_fusion), channel_id=1, replica_groups=mesh['loop'=16,'rep'=16] {'loop','rep'}, use_global_device_ids=true, to_apply=%region_8.11 | all-reduce | flops 256 | bytes 2048 | tf_op jit(solution)/shard_map/psum | solution.py:80
  349.7 177.0 %all-reduce.3.cloned.1.call-done = (f32[128,256]{0,1:T(8,128)}, f32[128,256]{1,0:T(8,128)}) async-done(((f32[128,256]{0,1:T(8,128)}, f32[128,256]{1,0:T(8,128)}), (f32[128,256]{0,1:T(8,128)}, f32[128,256]{1,0:T(8,128)})) %all-reduce.3.cloned.1.call-update) | async-done | bytes 262160 | tf_op jit(solution)/shard_map/psum | solution.py:80
  528.4 50.3 %all-gather.2.cloned.1.call-done = bf16[4096,128]{1,0:T(8,128)(2,1)} async-done(((bf16[256,128]{1,0:T(8,128)(2,1)}), bf16[4096,128]{1,0:T(8,128)(2,1)}) %all-gather.2.cloned.1.call-update) | async-done | bytes 1048592 | tf_op jit(solution)/shard_map/all_gather | solution.py:75
  583.2 112.8 %while.33 = (s32[]{:T(128)}, f32[256,128]{1,0:T(8,128)S(1)}, s32[]{:T(128)}, f32[16,16,2]{1,2,0:T(2,128)S(1)}, bf16[16,16,128,128]{3,2,1,0:T(8,128)(2,1)}, /*ind...) while((s32[]{:T(128)}, f32[256,128]{1,0:T(8,128)S(1)}, ...), condition=%wide.region_4.7_spmd, body=%wide.region_3.6_spmd.sunk | while | flops 73696368 | bytes 5510748 | solution.py:105
  583.2 3.4 collective-permute-start.1
  590.6 3.8 collective-permute-start.1
  598.5 3.1 collective-permute-start.1
  605.7 3.1 collective-permute-start.1
  620.1 3.5 collective-permute-start.1
  627.6 4.5 collective-permute-start.1
  636.1 3.6 collective-permute-start.1
  650.9 3.1 collective-permute-start.1
  665.3 3.8 collective-permute-start.1
  673.1 4.2 collective-permute-start.1
  681.3 3.4 collective-permute-start.1
  (281 shorter events, 173.0 us)
Async XLA Ops:
  7.2 262.9 %reduce-scatter.2.cloned.1.call-start = ((), (), s32[]{:S(2)}) async-start(), calls=%async_computation.1 | async-start | bytes 2228224 | tf_op jit(solution)/shard_map/reduce_scatter | solution.py:57
  14.8 9.2 %collective-permute-start = (bf16[256,128]{1,0:T(8,128)(2,1)S(1)}, bf16[256,128]{1,0:T(8,128)(2,1)S(1)}, u32[]{:S(2)}, u32[]{:S(2)}) collective-permute-start(bf16[256,128]{1,0:T(8,128)(2,1)S(1)} %get-tuple-element.526), channel_id=1, source_target_pairs={{240,0},{0,16},{16,32},{32,48},{48,64},{64,80},{80,96},{96,112},{1... | collective-permute-start | bytes 196616 | tf_op jit(solution)/shard_map/while/body/eval_jaxpr/ppermute | solution.py:11
  28.9 6.5 collective-permute-start
  40.3 6.5 collective-permute-start
  51.7 6.5 collective-permute-start
  63.1 6.5 collective-permute-start
  74.5 6.5 collective-permute-start
  85.8 6.5 collective-permute-start
  97.2 6.5 collective-permute-start
  108.6 7.0 collective-permute-start
  120.5 6.5 collective-permute-start
  143.3 6.5 collective-permute-start
  154.7 6.5 collective-permute-start
  166.1 6.5 collective-permute-start
  177.4 6.5 collective-permute-start
  191.4 335.3 %all-reduce.3.cloned.1.call-start = ((), (), s32[]{:S(2)}) async-start(), calls=%async_computation.3 | async-start | bytes 524288 | tf_op jit(solution)/shard_map/psum | solution.py:80
  273.9 304.7 %all-gather.2.cloned.1.call-start = ((), (), s32[]{:S(2)}) async-start(), calls=%async_computation.2 | async-start | bytes 1114112 | tf_op jit(solution)/shard_map/all_gather | solution.py:75
  583.2 7.4 %collective-permute-start.1 = (f32[256,128]{1,0:T(8,128)S(1)}, f32[256,128]{1,0:T(8,128)S(1)}, u32[]{:S(2)}, u32[]{:S(2)}) collective-permute-start(f32[256,128]{1,0:T(8,128)S(1)} %get-tuple-element.559), channel_id=1, source_target_pairs={{16,0},{32,16},{48,32},{64,48},{80,64},{96,80},{112,96},{128,112},... | collective-permute-start | bytes 393224 | tf_op jit(solution)/shard_map/while/body/eval_jaxpr/ppermute | solution.py:11
  590.6 7.8 %collective-permute-start.1 = (f32[256,128]{1,0:T(8,128)S(1)}, f32[256,128]{1,0:T(8,128)S(1)}, u32[]{:S(2)}, u32[]{:S(2)}) collective-permute-start(f32[256,128]{1,0:T(8,128)S(1)} %get-tuple-element.559), channel_id=1, source_target_pairs={{16,0},{32,16},{48,32},{64,48},{80,64},{96,80},{112,96},{128,112},... | collective-permute-start | bytes 393224 | tf_op jit(solution)/shard_map/while/body/eval_jaxpr/ppermute | solution.py:11
  598.5 7.1 %collective-permute-start.1 = (f32[256,128]{1,0:T(8,128)S(1)}, f32[256,128]{1,0:T(8,128)S(1)}, u32[]{:S(2)}, u32[]{:S(2)}) collective-permute-start(f32[256,128]{1,0:T(8,128)S(1)} %get-tuple-element.559), channel_id=1, source_target_pairs={{16,0},{32,16},{48,32},{64,48},{80,64},{96,80},{112,96},{128,112},... | collective-permute-start | bytes 393224 | tf_op jit(solution)/shard_map/while/body/eval_jaxpr/ppermute | solution.py:11
  605.7 7.1 %collective-permute-start.1 = (f32[256,128]{1,0:T(8,128)S(1)}, f32[256,128]{1,0:T(8,128)S(1)}, u32[]{:S(2)}, u32[]{:S(2)}) collective-permute-start(f32[256,128]{1,0:T(8,128)S(1)} %get-tuple-element.559), channel_id=1, source_target_pairs={{16,0},{32,16},{48,32},{64,48},{80,64},{96,80},{112,96},{128,112},... | collective-permute-start | bytes 393224 | tf_op jit(solution)/shard_map/while/body/eval_jaxpr/ppermute | solution.py:11
  612.9 7.1 %collective-permute-start.1 = (f32[256,128]{1,0:T(8,128)S(1)}, f32[256,128]{1,0:T(8,128)S(1)}, u32[]{:S(2)}, u32[]{:S(2)}) collective-permute-start(f32[256,128]{1,0:T(8,128)S(1)} %get-tuple-element.559), channel_id=1, source_target_pairs={{16,0},{32,16},{48,32},{64,48},{80,64},{96,80},{112,96},{128,112},... | collective-permute-start | bytes 393224 | tf_op jit(solution)/shard_map/while/body/eval_jaxpr/ppermute | solution.py:11
  620.1 7.5 %collective-permute-start.1 = (f32[256,128]{1,0:T(8,128)S(1)}, f32[256,128]{1,0:T(8,128)S(1)}, u32[]{:S(2)}, u32[]{:S(2)}) collective-permute-start(f32[256,128]{1,0:T(8,128)S(1)} %get-tuple-element.559), channel_id=1, source_target_pairs={{16,0},{32,16},{48,32},{64,48},{80,64},{96,80},{112,96},{128,112},... | collective-permute-start | bytes 393224 | tf_op jit(solution)/shard_map/while/body/eval_jaxpr/ppermute | solution.py:11
  627.6 8.5 %collective-permute-start.1 = (f32[256,128]{1,0:T(8,128)S(1)}, f32[256,128]{1,0:T(8,128)S(1)}, u32[]{:S(2)}, u32[]{:S(2)}) collective-permute-start(f32[256,128]{1,0:T(8,128)S(1)} %get-tuple-element.559), channel_id=1, source_target_pairs={{16,0},{32,16},{48,32},{64,48},{80,64},{96,80},{112,96},{128,112},... | collective-permute-start | bytes 393224 | tf_op jit(solution)/shard_map/while/body/eval_jaxpr/ppermute | solution.py:11
  636.1 7.6 %collective-permute-start.1 = (f32[256,128]{1,0:T(8,128)S(1)}, f32[256,128]{1,0:T(8,128)S(1)}, u32[]{:S(2)}, u32[]{:S(2)}) collective-permute-start(f32[256,128]{1,0:T(8,128)S(1)} %get-tuple-element.559), channel_id=1, source_target_pairs={{16,0},{32,16},{48,32},{64,48},{80,64},{96,80},{112,96},{128,112},... | collective-permute-start | bytes 393224 | tf_op jit(solution)/shard_map/while/body/eval_jaxpr/ppermute | solution.py:11
  643.7 7.1 %collective-permute-start.1 = (f32[256,128]{1,0:T(8,128)S(1)}, f32[256,128]{1,0:T(8,128)S(1)}, u32[]{:S(2)}, u32[]{:S(2)}) collective-permute-start(f32[256,128]{1,0:T(8,128)S(1)} %get-tuple-element.559), channel_id=1, source_target_pairs={{16,0},{32,16},{48,32},{64,48},{80,64},{96,80},{112,96},{128,112},... | collective-permute-start | bytes 393224 | tf_op jit(solution)/shard_map/while/body/eval_jaxpr/ppermute | solution.py:11
  650.9 7.1 %collective-permute-start.1 = (f32[256,128]{1,0:T(8,128)S(1)}, f32[256,128]{1,0:T(8,128)S(1)}, u32[]{:S(2)}, u32[]{:S(2)}) collective-permute-start(f32[256,128]{1,0:T(8,128)S(1)} %get-tuple-element.559), channel_id=1, source_target_pairs={{16,0},{32,16},{48,32},{64,48},{80,64},{96,80},{112,96},{128,112},... | collective-permute-start | bytes 393224 | tf_op jit(solution)/shard_map/while/body/eval_jaxpr/ppermute | solution.py:11
  658.1 7.1 %collective-permute-start.1 = (f32[256,128]{1,0:T(8,128)S(1)}, f32[256,128]{1,0:T(8,128)S(1)}, u32[]{:S(2)}, u32[]{:S(2)}) collective-permute-start(f32[256,128]{1,0:T(8,128)S(1)} %get-tuple-element.559), channel_id=1, source_target_pairs={{16,0},{32,16},{48,32},{64,48},{80,64},{96,80},{112,96},{128,112},... | collective-permute-start | bytes 393224 | tf_op jit(solution)/shard_map/while/body/eval_jaxpr/ppermute | solution.py:11
  665.3 7.8 %collective-permute-start.1 = (f32[256,128]{1,0:T(8,128)S(1)}, f32[256,128]{1,0:T(8,128)S(1)}, u32[]{:S(2)}, u32[]{:S(2)}) collective-permute-start(f32[256,128]{1,0:T(8,128)S(1)} %get-tuple-element.559), channel_id=1, source_target_pairs={{16,0},{32,16},{48,32},{64,48},{80,64},{96,80},{112,96},{128,112},... | collective-permute-start | bytes 393224 | tf_op jit(solution)/shard_map/while/body/eval_jaxpr/ppermute | solution.py:11
  673.1 8.2 %collective-permute-start.1 = (f32[256,128]{1,0:T(8,128)S(1)}, f32[256,128]{1,0:T(8,128)S(1)}, u32[]{:S(2)}, u32[]{:S(2)}) collective-permute-start(f32[256,128]{1,0:T(8,128)S(1)} %get-tuple-element.559), channel_id=1, source_target_pairs={{16,0},{32,16},{48,32},{64,48},{80,64},{96,80},{112,96},{128,112},... | collective-permute-start | bytes 393224 | tf_op jit(solution)/shard_map/while/body/eval_jaxpr/ppermute | solution.py:11
  681.3 7.4 %collective-permute-start.1 = (f32[256,128]{1,0:T(8,128)S(1)}, f32[256,128]{1,0:T(8,128)S(1)}, u32[]{:S(2)}, u32[]{:S(2)}) collective-permute-start(f32[256,128]{1,0:T(8,128)S(1)} %get-tuple-element.559), channel_id=1, source_target_pairs={{16,0},{32,16},{48,32},{64,48},{80,64},{96,80},{112,96},{128,112},... | collective-permute-start | bytes 393224 | tf_op jit(solution)/shard_map/while/body/eval_jaxpr/ppermute | solution.py:11
  688.8 7.1 %collective-permute-start.1 = (f32[256,128]{1,0:T(8,128)S(1)}, f32[256,128]{1,0:T(8,128)S(1)}, u32[]{:S(2)}, u32[]{:S(2)}) collective-permute-start(f32[256,128]{1,0:T(8,128)S(1)} %get-tuple-element.559), channel_id=1, source_target_pairs={{16,0},{32,16},{48,32},{64,48},{80,64},{96,80},{112,96},{128,112},... | collective-permute-start | bytes 393224 | tf_op jit(solution)/shard_map/while/body/eval_jaxpr/ppermute | solution.py:11
  (11 other events, 551.8 us)
Sparse Core Ops, SparseCore 0:
  191.5 78.5 reduce-scatter.1
  276.3 250.3 all-reduce.2
  530.0 48.5 all-gather.1
where the time goes:
time: 706 us; the launch traced here: 704 us
  waiting for transfers between devices  401 us (57%)
  matrix products  114 us (16%)
  blocking collectives  74.1 us (10%)
  starting transfers between devices  55.1 us (8%)
  local copies, waits for them, and re-layouts  29.7 us (4%)
  other arithmetic  14.1 us (2%)
  between operations  13.9 us (2%)
    psum x1, waiting for transfers between devices, per_device(): lax.psum((jnp.einsum('nf,nh->fh', features, grad_pre, preferred_element_t...  177 us
    ppermute x30, waiting for transfers between devices, shifted(): return lax.ppermute(block, axis, route)  96.3 us
    reduce_scatter x1, waiting for transfers between devices, per_device(): lax.psum_scatter(running.reshape(row_blocks * tile_size, feat_width), 're...  77.7 us
    psum x1, blocking collectives, per_device(): lax.psum((jnp.einsum('nf,nh->fh', features, grad_pre, preferred_element_t...  74.1 us
    ppermute x30, starting transfers between devices, shifted(): return lax.ppermute(block, axis, route)  55 us
    all_gather x1, waiting for transfers between devices, per_device(): lax.all_gather(grad_agg, 'rep', axis=0, tiled=True)  50.3 us
    dot_general x16, matrix products, gather_term(): jnp.einsum('td,tif->dif', pick_entry(place_all, source), product, precisi...  43.8 us
    dot_general x16, matrix products, spread_term(): jnp.einsum('tij,tif->tjf', tile_part, chosen, preferred_element_type=jnp....  22.8 us
  transfers between devices with their start and end apart: 33, of which 18 were waited for; matrix products, arithmetic and copies ran while one was open for 9% of the time, Pallas kernels for 0%

commit v1 on v0

--- a/solution.py
+++ b/solution.py
@@ -78,14 +78,17 @@
     node_total = row_count * loop_count * rep_count
     grad_scale = 1.0 / math.sqrt(node_total)
     grad_self, grad_neigh, grad_bias = lax.psum(
-        (
-            jnp.einsum("nf,nh->fh", features, grad_pre, preferred_element_type=jnp.float32)
-            * grad_scale,
-            jnp.einsum("nf,nh->fh", aggregate, grad_pre, preferred_element_type=jnp.float32)
-            * grad_scale,
-            jnp.sum(grad_pre.astype(jnp.float32), axis=0) * grad_scale,
+        lax.psum(
+            (
+                jnp.einsum("nf,nh->fh", features, grad_pre, preferred_element_type=jnp.float32)
+                * grad_scale,
+                jnp.einsum("nf,nh->fh", aggregate, grad_pre, preferred_element_type=jnp.float32)
+                * grad_scale,
+                jnp.sum(grad_pre.astype(jnp.float32), axis=0) * grad_scale,
+            ),
+            "loop",
         ),
-        ("loop", "rep"),
+        "rep",
     )
     self_grad = jnp.einsum("nh,fh->nf", grad_pre, w_self, preferred_element_type=jnp.float32)
 

time: 706 us -> 737 us (1.044)
  waiting for transfers between devices: 401 us -> 443 us
  blocking collectives: 74.1 us -> 62.9 us
    psum x0 -> x1, waiting for transfers between devices: none -> 76.4 us  [per_device(): lax.psum(lax.psum((jnp.einsum('nf,nh->fh', features, grad_pre, preferred_...]
    psum x1, waiting for transfers between devices: 177 us -> 136 us  [per_device(): lax.psum((jnp.einsum('nf,nh->fh', features, grad_pre, preferred_element_t...]
    psum x1, blocking collectives: 74.1 us -> 34.3 us  [per_device(): lax.psum((jnp.einsum('nf,nh->fh', features, grad_pre, preferred_element_t...]
    psum x0 -> x1, blocking collectives: none -> 28.6 us  [per_device(): lax.psum(lax.psum((jnp.einsum('nf,nh->fh', features, grad_pre, preferred_...]
  transfers between devices with their start and end apart: 33 -> 34, of which waited for: 18 -> 19; matrix products, arithmetic and copies ran while one was open for 9% -> 9% of each run, Pallas kernels for 0% -> 0%
where the time goes in v1:
time: 737 us; the launch traced here: 735 us
  waiting for transfers between devices  443 us (60%)
  matrix products  114 us (15%)
  blocking collectives  62.9 us (9%)
  starting transfers between devices  55.1 us (7%)
  local copies, waits for them, and re-layouts  29.7 us (4%)
  other arithmetic  14.1 us (2%)
  between operations  14 us (2%)
    psum x1, waiting for transfers between devices, per_device(): lax.psum((jnp.einsum('nf,nh->fh', features, grad_pre, preferred_element_t...  136 us
    ppermute x30, waiting for transfers between devices, shifted(): return lax.ppermute(block, axis, route)  96.3 us
    reduce_scatter x1, waiting for transfers between devices, per_device(): lax.psum_scatter(running.reshape(row_blocks * tile_size, feat_width), 're...  77.7 us
    psum x1, waiting for transfers between devices, per_device(): lax.psum(lax.psum((jnp.einsum('nf,nh->fh', features, grad_pre, preferred_...  76.4 us
    all_gather x1, waiting for transfers between devices, per_device(): lax.all_gather(grad_agg, 'rep', axis=0, tiled=True)  57.2 us
    ppermute x30, starting transfers between devices, shifted(): return lax.ppermute(block, axis, route)  55 us
    dot_general x16, matrix products, gather_term(): jnp.einsum('td,tif->dif', pick_entry(place_all, source), product, precisi...  43.8 us
    psum x1, blocking collectives, per_device(): lax.psum((jnp.einsum('nf,nh->fh', features, grad_pre, preferred_element_t...  34.3 us
  transfers between devices with their start and end apart: 34, of which 19 were waited for; matrix products, arithmetic and copies ran while one was open for 9% of the time, Pallas kernels for 0%

profile of v1, /device:TPU:2, one launch (start us, length us, event | category | flops | bytes accessed | tf_op | source)
XLA Modules:
  0.0 734.8 jit_solution(15743574629431847141)
XLA Ops:
  14.8 174.0 %while.32 = (s32[]{:T(128)}, bf16[256,128]{1,0:T(8,128)(2,1)S(1)}, f32[32,128,128]{2,0,1:T(8,128)S(1)}, s32[]{:T(128)}, f32[16,16,32]{2,1,0:T(8,128)S(1)}, /*ind...) while((s32[]{:T(128)}, bf16[256,128]{1,0:T(8,128)(2,1)S(1)}, ...), condition=%wide.region_1.3_spmd, body=%wide.region_0.2_spmd.sunk | while | flops 168559728 | bytes 8794716 | solution.py:56
  16.5 7.5 %collective-permute-done = bf16[256,128]{1,0:T(8,128)(2,1)S(1)} collective-permute-done((bf16[256,128]{1,0:T(8,128)(2,1)S(1)}, bf16[256,128]{1,0:T(8,128)(2,1)S(1)}, u32[]{:S(2)}, u32[]{:S(2)}) %collective-permute-start) | collective-permute-done | bytes 65568 | tf_op jit(solution)/shard_map/while/body/eval_jaxpr/ppermute | solution.py:11
  29.1 6.3 collective-permute-done
  40.5 6.3 collective-permute-done
  51.8 6.3 collective-permute-done
  63.2 6.3 collective-permute-done
  74.6 6.3 collective-permute-done
  86.0 6.3 collective-permute-done
  97.4 6.3 collective-permute-done
  108.8 6.8 collective-permute-done
  120.7 6.3 collective-permute-done
  132.0 6.3 collective-permute-done
  143.4 6.3 collective-permute-done
  154.8 6.3 collective-permute-done
  166.2 6.3 collective-permute-done
  177.6 6.3 collective-permute-done
  192.4 77.7 %reduce-scatter.2.cloned.1.call-done = f32[256,128]{1,0:T(8,128)} async-done(((f32[4096,128]{1,0:T(8,128)}), f32[256,128]{1,0:T(8,128)}) %reduce-scatter.2.cloned.1.call-update) | async-done | bytes 131088 | tf_op jit(solution)/shard_map/reduce_scatter | solution.py:57
  274.0 135.7 %all-reduce.7.cloned.1.call-done = (f32[128,256]{0,1:T(8,128)}, f32[128,256]{1,0:T(8,128)}) async-done(((f32[128,256]{0,1:T(8,128)}, f32[128,256]{1,0:T(8,128)}), (f32[128,256]{0,1:T(8,128)}, f32[128,256]{1,0:T(8,128)})) %all-reduce.7.cloned.1.call-update) | async-done | bytes 262160 | tf_op jit(solution)/shard_map/psum | solution.py:81
  411.3 34.3 %psum.46 = f32[256]{0:T(256)S(1)} all-reduce(f32[256]{0:T(256)S(1)} %broadcast_multiply_fusion), channel_id=1, replica_groups=mesh['loop'=16,'rep'=16] {'loop'}, use_global_device_ids=true, to_apply=%region_10.13 | all-reduce | flops 256 | bytes 2048 | tf_op jit(solution)/shard_map/psum | solution.py:81
  445.6 28.6 %psum.47 = f32[256]{0:T(256)} all-reduce(f32[256]{0:T(256)S(1)} %psum.46), channel_id=1, replica_groups=mesh['loop'=16,'rep'=16] {'rep'}, use_global_device_ids=true, to_apply=%region_11.14 | all-reduce | flops 256 | bytes 2048 | tf_op jit(solution)/shard_map/psum | solution.py:80
  474.2 76.4 %all-reduce.5.cloned.1.call-done = (f32[128,256]{0,1:T(8,128)}, f32[128,256]{1,0:T(8,128)}) async-done(((f32[128,256]{0,1:T(8,128)}, f32[128,256]{1,0:T(8,128)}), (f32[128,256]{0,1:T(8,128)}, f32[128,256]{1,0:T(8,128)})) %all-reduce.5.cloned.1.call-update) | async-done | bytes 262160 | tf_op jit(solution)/shard_map/psum | solution.py:80
  552.2 57.2 %all-gather.2.cloned.1.call-done = bf16[4096,128]{1,0:T(8,128)(2,1)} async-done(((bf16[256,128]{1,0:T(8,128)(2,1)}), bf16[4096,128]{1,0:T(8,128)(2,1)}) %all-gather.2.cloned.1.call-update) | async-done | bytes 1048592 | tf_op jit(solution)/shard_map/all_gather | solution.py:75
  614.0 112.8 %while.33 = (s32[]{:T(128)}, f32[256,128]{1,0:T(8,128)S(1)}, s32[]{:T(128)}, f32[16,16,2]{1,2,0:T(2,128)S(1)}, bf16[16,16,128,128]{3,2,1,0:T(8,128)(2,1)}, /*ind...) while((s32[]{:T(128)}, f32[256,128]{1,0:T(8,128)S(1)}, ...), condition=%wide.region_4.7_spmd, body=%wide.region_3.6_spmd.sunk | while | flops 73696368 | bytes 5510748 | solution.py:108
  614.0 3.4 collective-permute-start.1
  621.5 3.8 collective-permute-start.1
  650.9 3.5 collective-permute-start.1
  658.4 4.5 collective-permute-start.1
  666.9 3.6 collective-permute-start.1
  681.8 3.1 collective-permute-start.1
  696.1 3.8 collective-permute-start.1
  703.9 4.2 collective-permute-start.1
  712.2 3.4 collective-permute-start.1
  (285 shorter events, 179.3 us)
Async XLA Ops:
  7.2 262.9 %reduce-scatter.2.cloned.1.call-start = ((), (), s32[]{:S(2)}) async-start(), calls=%async_computation.1 | async-start | bytes 2228224 | tf_op jit(solution)/shard_map/reduce_scatter | solution.py:57
  14.8 9.2 %collective-permute-start = (bf16[256,128]{1,0:T(8,128)(2,1)S(1)}, bf16[256,128]{1,0:T(8,128)(2,1)S(1)}, u32[]{:S(2)}, u32[]{:S(2)}) collective-permute-start(bf16[256,128]{1,0:T(8,128)(2,1)S(1)} %get-tuple-element.528), channel_id=1, source_target_pairs={{240,0},{0,16},{16,32},{32,48},{48,64},{64,80},{80,96},{96,112},{1... | collective-permute-start | bytes 196616 | tf_op jit(solution)/shard_map/while/body/eval_jaxpr/ppermute | solution.py:11
  28.9 6.5 collective-permute-start
  40.3 6.5 collective-permute-start
  51.7 6.5 collective-permute-start
  63.1 6.5 collective-permute-start
  85.8 6.5 collective-permute-start
  97.2 6.5 collective-permute-start
  108.6 7.0 collective-permute-start
  120.5 6.5 collective-permute-start
  143.3 6.5 collective-permute-start
  154.7 6.5 collective-permute-start
  166.1 6.5 collective-permute-start
  177.4 6.5 collective-permute-start
  191.4 218.2 %all-reduce.7.cloned.1.call-start = ((), (), s32[]{:S(2)}) async-start(), calls=%async_computation.4 | async-start | bytes 524288 | tf_op jit(solution)/shard_map/psum | solution.py:81
  273.9 276.6 %all-reduce.5.cloned.1.call-start = ((), (), s32[]{:S(2)}) async-start(), calls=%async_computation.3 | async-start | bytes 524288 | tf_op jit(solution)/shard_map/psum | solution.py:80
  409.7 199.8 %all-gather.2.cloned.1.call-start = ((), (), s32[]{:S(2)}) async-start(), calls=%async_computation.2 | async-start | bytes 1114112 | tf_op jit(solution)/shard_map/all_gather | solution.py:75
  614.0 7.4 %collective-permute-start.1 = (f32[256,128]{1,0:T(8,128)S(1)}, f32[256,128]{1,0:T(8,128)S(1)}, u32[]{:S(2)}, u32[]{:S(2)}) collective-permute-start(f32[256,128]{1,0:T(8,128)S(1)} %get-tuple-element.561), channel_id=1, source_target_pairs={{16,0},{32,16},{48,32},{64,48},{80,64},{96,80},{112,96},{128,112},... | collective-permute-start | bytes 393224 | tf_op jit(solution)/shard_map/while/body/eval_jaxpr/ppermute | solution.py:11
  621.5 7.8 %collective-permute-start.1 = (f32[256,128]{1,0:T(8,128)S(1)}, f32[256,128]{1,0:T(8,128)S(1)}, u32[]{:S(2)}, u32[]{:S(2)}) collective-permute-start(f32[256,128]{1,0:T(8,128)S(1)} %get-tuple-element.561), channel_id=1, source_target_pairs={{16,0},{32,16},{48,32},{64,48},{80,64},{96,80},{112,96},{128,112},... | collective-permute-start | bytes 393224 | tf_op jit(solution)/shard_map/while/body/eval_jaxpr/ppermute | solution.py:11
  629.3 7.1 collective-permute-start.1
  636.5 7.1 collective-permute-start.1
  643.7 7.1 collective-permute-start.1
  650.9 7.5 %collective-permute-start.1 = (f32[256,128]{1,0:T(8,128)S(1)}, f32[256,128]{1,0:T(8,128)S(1)}, u32[]{:S(2)}, u32[]{:S(2)}) collective-permute-start(f32[256,128]{1,0:T(8,128)S(1)} %get-tuple-element.561), channel_id=1, source_target_pairs={{16,0},{32,16},{48,32},{64,48},{80,64},{96,80},{112,96},{128,112},... | collective-permute-start | bytes 393224 | tf_op jit(solution)/shard_map/while/body/eval_jaxpr/ppermute | solution.py:11
  658.4 8.5 %collective-permute-start.1 = (f32[256,128]{1,0:T(8,128)S(1)}, f32[256,128]{1,0:T(8,128)S(1)}, u32[]{:S(2)}, u32[]{:S(2)}) collective-permute-start(f32[256,128]{1,0:T(8,128)S(1)} %get-tuple-element.561), channel_id=1, source_target_pairs={{16,0},{32,16},{48,32},{64,48},{80,64},{96,80},{112,96},{128,112},... | collective-permute-start | bytes 393224 | tf_op jit(solution)/shard_map/while/body/eval_jaxpr/ppermute | solution.py:11
  666.9 7.6 %collective-permute-start.1 = (f32[256,128]{1,0:T(8,128)S(1)}, f32[256,128]{1,0:T(8,128)S(1)}, u32[]{:S(2)}, u32[]{:S(2)}) collective-permute-start(f32[256,128]{1,0:T(8,128)S(1)} %get-tuple-element.561), channel_id=1, source_target_pairs={{16,0},{32,16},{48,32},{64,48},{80,64},{96,80},{112,96},{128,112},... | collective-permute-start | bytes 393224 | tf_op jit(solution)/shard_map/while/body/eval_jaxpr/ppermute | solution.py:11
  674.6 7.1 collective-permute-start.1
  681.8 7.1 collective-permute-start.1
  689.0 7.1 collective-permute-start.1
  696.1 7.8 %collective-permute-start.1 = (f32[256,128]{1,0:T(8,128)S(1)}, f32[256,128]{1,0:T(8,128)S(1)}, u32[]{:S(2)}, u32[]{:S(2)}) collective-permute-start(f32[256,128]{1,0:T(8,128)S(1)} %get-tuple-element.561), channel_id=1, source_target_pairs={{16,0},{32,16},{48,32},{64,48},{80,64},{96,80},{112,96},{128,112},... | collective-permute-start | bytes 393224 | tf_op jit(solution)/shard_map/while/body/eval_jaxpr/ppermute | solution.py:11
  703.9 8.2 %collective-permute-start.1 = (f32[256,128]{1,0:T(8,128)S(1)}, f32[256,128]{1,0:T(8,128)S(1)}, u32[]{:S(2)}, u32[]{:S(2)}) collective-permute-start(f32[256,128]{1,0:T(8,128)S(1)} %get-tuple-element.561), channel_id=1, source_target_pairs={{16,0},{32,16},{48,32},{64,48},{80,64},{96,80},{112,96},{128,112},... | collective-permute-start | bytes 393224 | tf_op jit(solution)/shard_map/while/body/eval_jaxpr/ppermute | solution.py:11
  712.2 7.4 %collective-permute-start.1 = (f32[256,128]{1,0:T(8,128)S(1)}, f32[256,128]{1,0:T(8,128)S(1)}, u32[]{:S(2)}, u32[]{:S(2)}) collective-permute-start(f32[256,128]{1,0:T(8,128)S(1)} %get-tuple-element.561), channel_id=1, source_target_pairs={{16,0},{32,16},{48,32},{64,48},{80,64},{96,80},{112,96},{128,112},... | collective-permute-start | bytes 393224 | tf_op jit(solution)/shard_map/while/body/eval_jaxpr/ppermute | solution.py:11
  719.6 7.1 collective-permute-start.1
  (12 other events, 558.2 us)
Sparse Core Ops, SparseCore 0:
  191.5 78.5 reduce-scatter.1
  274.1 135.5 all-reduce.6
  412.5 138.0 all-reduce.4
  553.8 55.6 all-gather.1
